TPU v7x, 32 devices: a whole 2x2x4 slice. The times are simulated.
32 devices in a mesh: strike: 8 (over y, x, core), dip: 4 (over z).
Axes of the slice: x: 2, y: 2, z: 4, core: 2. Of those that a mesh axis runs over, the one named last changes fastest.
Arguments:
- adjoint_state: float32 [9, 64, 64, 128], P(None, 'strike', 'dip'), may hold values from -6 to 6
- lame_lambda: float32 [64, 64, 128], P('strike', 'dip'), may hold values from 0.5 to 2
- lame_mu: float32 [64, 64, 128], P('strike', 'dip'), may hold values from 0.3 to 1.5
- buoyancy: float32 [64, 64, 128], P('strike', 'dip'), may hold values from 0.5 to 2
- residual: bfloat16 [16384, 3, 128], P(('strike', 'dip')), may hold values from -6 to 6
- receiver_tile: int32 [16384, 1], P(('strike', 'dip')), may hold values from 0 to 31; in each aligned block of 512 rows (0 to 511, 512 to 1023, ...) at most 32 rows name the same one
- receiver_cell: int32 [16384], P(('strike', 'dip')), may hold values from 0 to 16383, as said below
- resample: float32 [2, 128], replicated, may hold values from -0.5 to 0.5
- fault_patch: int32 [32, 256], P(('strike', 'dip')), may hold values from 0 to 2047, as said below
- fault_cell: int32 [32, 256], P(('strike', 'dip')), may hold values from 0 to 16383, as said below
- fault_area: float32 [32, 256], P(('strike', 'dip')), may hold values from 0.25 to 1
- moment: float32 [6, 2048], replicated, may hold values from -6 to 6
- subpatch_order: int32 [2048], replicated, may hold values from 0 to 2047, each once
Outputs:
- adjoint_out: float32 [9, 64, 64, 128], P(None, 'strike', 'dip')
- slip_gradient: float32 [2, 2048], P(None, ('strike', 'dip'))
Inputs may be any that keep to these rules, and one draw needn't show every extreme that they name: `receiver_tile`: tile t is the device at index t of strike+dip. In the rows of one device at most 32 stations name the same tile. `receiver_cell`: cell of the station within the block of tile receiver_tile. `fault_patch`: the entries of tile t name subpatches within 132 of t * 64, counted cyclically. `fault_cell`: cell of the entry within the block of the tile of its row.
All inputs are finite; a program needn't handle non-finite values.
Results may differ from a plain program's by a relative error of at most 0.0003.
Values may be sent and summed in bfloat16 or wider, within the bound.
A program may use at most 64 MiB of HBM per device.

v0:
```python
import jax
import jax.numpy as jnp
from jax import lax
from jax.sharding import PartitionSpec as P

STEPS = 2


time_step = 0.25


def with_halo(cells, sides, width):
    for axis, dim in sides:
        count = lax.axis_size(axis)
        ends = count - 1
        head = lax.slice_in_dim(cells, 0, width, axis=dim)
        tail = lax.slice_in_dim(cells, cells.shape[dim] - width, cells.shape[dim], axis=dim)
        cells = jnp.concatenate(
            [
                lax.ppermute(tail, axis, [(i, (i + 1) % count) for i in range(ends)]),
                cells,
                lax.ppermute(head, axis, [((i + 1) % count, i) for i in range(ends)]),
            ],
            axis=dim,
        )
    return cells


def derivatives(padded):
    along_x = (padded[:, 2:, 1:-1, 1:-1] - padded[:, :-2, 1:-1, 1:-1]) * 0.5
    along_y = (padded[:, 1:-1, 2:, 1:-1] - padded[:, 1:-1, :-2, 1:-1]) * 0.5
    along_z = (padded[:, 1:-1, 1:-1, 2:] - padded[:, 1:-1, 1:-1, :-2]) * 0.5
    return (along_x, along_y, along_z)


def velocity_update(velocity, stress_padded, source, buoyancy):
    along_x, along_y, along_z = derivatives(stress_padded)
    force_x = along_x[0] + along_y[3] + along_z[4]
    force_y = along_x[3] + along_y[1] + along_z[5]
    force_z = along_x[4] + along_y[5] + along_z[2]
    return velocity + time_step * (buoyancy * jnp.stack([force_x, force_y, force_z]) + source)


def stress_update(stress, velocity_padded, lame_lambda, lame_mu):
    along_x, along_y, along_z = derivatives(velocity_padded)
    dilation = along_x[0] + along_y[1] + along_z[2]
    return jnp.stack(
        [
            stress[0] + time_step * (lame_lambda * dilation + 2.0 * lame_mu * along_x[0]),
            stress[1] + time_step * (lame_lambda * dilation + 2.0 * lame_mu * along_y[1]),
            stress[2] + time_step * (lame_lambda * dilation + 2.0 * lame_mu * along_z[2]),
            stress[3] + time_step * lame_mu * (along_y[0] + along_x[1]),
            stress[4] + time_step * lame_mu * (along_z[0] + along_x[2]),
            stress[5] + time_step * lame_mu * (along_z[1] + along_y[2]),
        ]
    )


def pad_depth(field):
    return jnp.pad(field, ((0, 0), (0, 0), (0, 0), (1, 1)))


def shards(
    adjoint_state,
    lame_lambda,
    lame_mu,
    buoyancy,
    residual,
    receiver_tile,
    receiver_cell,
    resample,
    fault_patch,
    fault_cell,
    fault_area,
    moment,
    subpatch_order,
):
    strike_count = lax.axis_size("strike")
    dip_count = lax.axis_size("dip")
    tile_count = strike_count * dip_count
    station_count = residual.shape[0]
    slot_count = max(2, (2 * station_count + tile_count - 1) // tile_count)
    local_x, local_y, local_z = buoyancy.shape
    cell_total = local_x * local_y * local_z
    targets = receiver_tile[:, 0]
    order_ids = jnp.arange(station_count, dtype=jnp.int32)
    matches = (targets[:, None] == targets[None, :]) & (order_ids[None, :] < order_ids[:, None])
    ordinal = jnp.sum(matches.astype(jnp.int32), axis=1)
    slot_index = targets * slot_count + ordinal
    cell_list = jnp.zeros((tile_count * slot_count,), jnp.int32).at[slot_index].set(receiver_cell)
    cell_list = cell_list.reshape(strike_count, dip_count, slot_count)
    payload = residual.reshape(station_count, -1)
    outgoing = (
        jnp.zeros((tile_count * slot_count, payload.shape[1]), jnp.bfloat16)
        .at[slot_index]
        .set(payload)
    )
    outgoing = outgoing.reshape(strike_count, dip_count, slot_count, -1)
    arrived, arrived_cells = (
        lax.all_to_all(
            lax.all_to_all(outgoing, "strike", split_axis=0, concat_axis=0, tiled=True),
            "dip",
            split_axis=1,
            concat_axis=1,
            tiled=True,
        ),
        lax.all_to_all(
            lax.all_to_all(cell_list, "strike", split_axis=0, concat_axis=0, tiled=True),
            "dip",
            split_axis=1,
            concat_axis=1,
            tiled=True,
        ),
    )
    traces = arrived.reshape(-1, 3, resample.shape[1]).astype(jnp.float32)
    amplitude = jnp.einsum("rct,kt->krc", traces, resample, precision=lax.Precision.HIGHEST)
    arrived_cells = arrived_cells.reshape(-1)
    patch_ids = fault_patch[0]
    sample_cells = fault_cell[0]
    areas = fault_area[0]
    pattern = moment[:, patch_ids]
    velocity = adjoint_state[0:3]
    stress = adjoint_state[3:9]
    partials = []
    for step in range(STEPS):
        source = jnp.zeros((3, cell_total), jnp.float32).at[:, arrived_cells].add(amplitude[step].T)
        source = source.reshape(3, local_x, local_y, local_z)
        stress_wide = with_halo(stress, (("strike", 1), ("dip", 2)), 1)
        velocity = velocity_update(velocity, pad_depth(stress_wide), source, buoyancy)
        velocity_wide = with_halo(velocity, (("strike", 1), ("dip", 2)), 1)
        stress = stress_update(stress, pad_depth(velocity_wide), lame_lambda, lame_mu)
        sampled = stress.reshape(6, -1)[:, sample_cells]
        contrib = areas * jnp.sum(pattern * sampled, axis=0)
        partial_sum = jnp.zeros((moment.shape[1],), jnp.float32).at[patch_ids].add(contrib)
        partials.append(partial_sum[subpatch_order])
    gathered = jnp.stack(partials)
    sectioned = gathered.reshape(STEPS, strike_count, -1)
    first_sum = lax.psum_scatter(sectioned, "strike", scatter_dimension=1, tiled=True)
    slip_gradient = lax.psum_scatter(first_sum, "dip", scatter_dimension=2, tiled=True).reshape(
        STEPS, -1
    )
    return (jnp.concatenate([velocity, stress]), slip_gradient)


def solution(mesh):
    return jax.shard_map(
        shards,
        mesh=mesh,
        in_specs=(
            P(None, "strike", "dip", None),
            P("strike", "dip", None),
            P("strike", "dip", None),
            P("strike", "dip", None),
            P(("strike", "dip"), None, None),
            P(("strike", "dip"), None),
            P(("strike", "dip")),
            P(),
            P(("strike", "dip"), None),
            P(("strike", "dip"), None),
            P(("strike", "dip"), None),
            P(),
            P(),
        ),
        out_specs=(P(None, "strike", "dip", None), P(None, ("strike", "dip"))),
        check_vma=False,
    )
```

profile of v0, /device:TPU:0, one launch (start us, length us, event | category | flops | bytes accessed | tf_op | source)
XLA Modules:
  0.0 252.2 jit_solution(10685988677493331242)
XLA Ops:
  7.2 1.0 convert_reduce_fusion
  8.2 0.7 compare_select_fusion.2
  8.9 2.6 %scatter_custom_fusion = s32[1024]{0:T(1024)S(1)} fusion(s32[512]{0:T(512)S(1)} %bitcast.216, s32[512]{0:T(512)} %param.19, s32[]{:T(128)} %constant.12.clone.1), kind=kCustom, calls=%fused_computation.200 | custom fusion | bytes 4608 | tf_op jit(solution)/shard_map/scatter | solution.py:90
  11.6 0.7 reshape.266
  12.2 5.2 %all-to-all-start = ((s32[8,1,128]{2,1,0:T(1,128)}), s32[8,1,128]{2,1,0:T(1,128)S(1)}, u32[]{:S(2)}, u32[]{:S(2)}) async-start(s32[8,1,128]{2,1,0:T(1,128)} %reshape.266), calls=%async_computation | async-start | bytes 8192 | tf_op jit(solution)/shard_map/all_to_all | solution.py:108
  17.4 1.2 copy.101
  18.8 3.3 %scatter_custom_fusion.1 = bf16[1024,384]{1,0:T(8,128)(2,1)} fusion(s32[512]{0:T(512)S(1)} %bitcast.217, bf16[512,384]{1,0:T(8,128)(2,1)S(1)} %copy.102, bf16[]{:T(256)} %constant.16.clone.1), kind=kCustom, calls=%fused_computation.72 | custom fusion | bytes 786434 | tf_op jit(solution)/shard_map/scatter | solution.py:96
  22.2 4.2 %all-to-all-start.2 = ((bf16[8,4,32,384]{3,2,1,0:T(8,128)(2,1)}), bf16[8,4,32,384]{3,2,1,0:T(8,128)(2,1)S(1)}, u32[]{:S(2)}, u32[]{:S(2)}) async-start(bf16[8,4,32,384]{3,2,1,0:T(8,128)(2,1)} %bitcast.5), calls=%async_computation.2 | async-start | bytes 1572864 | tf_op jit(solution)/shard_map/all_to_all | solution.py:101
  26.4 0.5 broadcast.280
  26.9 0.7 reduce.2
  27.6 0.7 reshape.268
  28.3 10.6 %all-to-all-done.2 = bf16[8,4,32,384]{3,2,1,0:T(8,128)(2,1)S(1)} async-done(((bf16[8,4,32,384]{3,2,1,0:T(8,128)(2,1)}), bf16[8,4,32,384]{3,2,1,0:T(8,128)(2,1)S(1)}, u32[]{:S(2)}, u32[]{:S(2)}) %all-to-all-start.2) | async-done | bytes 786464 | tf_op jit(solution)/shard_map/all_to_all | solution.py:101
  38.9 4.9 %all-to-all-start.1 = ((s32[4,1,256]{2,1,0:T(1,128)}), s32[4,1,256]{2,1,0:T(1,128)S(1)}, u32[]{:S(2)}, u32[]{:S(2)}) async-start(s32[4,1,256]{2,1,0:T(1,128)} %reshape.268), calls=%async_computation.1 | async-start | bytes 8192 | tf_op jit(solution)/shard_map/all_to_all | solution.py:107
  43.8 1.0 copy.103
  44.8 4.6 %all-to-all-done.1 = s32[4,1,256]{2,1,0:T(1,128)S(1)} async-done(((s32[4,1,256]{2,1,0:T(1,128)}), s32[4,1,256]{2,1,0:T(1,128)S(1)}, u32[]{:S(2)}, u32[]{:S(2)}) %all-to-all-start.1) | async-done | bytes 4128 | tf_op jit(solution)/shard_map/all_to_all | solution.py:107
  49.4 3.5 %all-to-all-start.3 = ((bf16[8,4,32,384]{3,2,0,1:T(8,128)(2,1)}), bf16[8,4,32,384]{3,2,0,1:T(8,128)(2,1)S(1)}, u32[]{:S(2)}, u32[]{:S(2)}) async-start(bf16[8,4,32,384]{3,2,0,1:T(8,128)(2,1)} %copy.103), calls=%async_computation.3 | async-start | bytes 1572864 | tf_op jit(solution)/shard_map/all_to_all | solution.py:100
  53.0 1.3 collective-permute-start
  54.3 3.0 %collective-permute-start.1 = (f32[6,1,16,128]{3,2,1,0:T(8,128)S(1)}, f32[6,1,16,128]{3,2,1,0:T(8,128)S(1)}, u32[]{:S(2)}, u32[]{:S(2)}) collective-permute-start(f32[6,1,16,128]{3,2,1,0:T(8,128)S(1)} %get-tuple-element.38), channel_id=1, source_target_pairs={{0,4},{4,8},{8,12},{12,16},{16,20},{20,24},{24,28},{1,5},{5,9},{9,... | collective-permute-start | bytes 147464 | tf_op jit(solution)/shard_map/ppermute | solution.py:20
  57.3 0.7 reduce.3
  58.2 1.3 collective-permute-start.2
  59.5 4.5 %collective-permute-start.3 = (f32[6,10,1,128]{3,2,1,0:T(1,128)S(1)}, f32[6,10,1,128]{3,2,1,0:T(1,128)S(1)}, u32[]{:S(2)}, u32[]{:S(2)}) collective-permute-start(f32[6,10,1,128]{3,2,1,0:T(1,128)S(1)} %get-tuple-element.46), channel_id=1, source_target_pairs={{0,1},{1,2},{2,3},{4,5},{5,6},{6,7},{8,9},{9,10},{10,11},{12,13},{... | collective-permute-start | bytes 92168 | tf_op jit(solution)/shard_map/ppermute | solution.py:20
  64.2 1.4 collective-permute-done.3
  65.7 0.7 select_maximum_fusion.4
  66.7 2.6 %all-to-all-done.3 = bf16[8,4,32,384]{3,2,0,1:T(8,128)(2,1)S(1)} async-done(((bf16[8,4,32,384]{3,2,0,1:T(8,128)(2,1)}), bf16[8,4,32,384]{3,2,0,1:T(8,128)(2,1)S(1)}, u32[]{:S(2)}, u32[]{:S(2)}) %all-to-all-start.3) | async-done | bytes 786464 | tf_op jit(solution)/shard_map/all_to_all | solution.py:100
  69.8 0.7 convolution_bitcast_fusion
  70.7 9.9 %scatter_custom_fusion.2 = f32[3,16384]{0,1:T(8,128)} fusion(s32[1024]{0:T(1024)S(1)} %bitcast.214, f32[]{:T(128)} %constant.11.clone.1, f32[1,1024,3]{2,1,0:T(8,128)S(1)} %copy.113), kind=kCustom, calls=%fused_computation.13 | custom fusion | flops 3072 | bytes 720900 | tf_op jit(solution)/shard_map/scatter-add | solution.py:126
  80.7 5.3 %copy.107 = f32[3,8,16,128]{3,2,1,0:T(8,128)S(1)} copy(f32[3,8,16,128]{0,3,2,1:T(8,128)} %bitcast.188) | data formatting | bytes 393216 | tf_op jit(solution)/shard_map/reshape | solution.py:127
  86.0 1.4 collective-permute-start.4
  87.5 3.0 %collective-permute-start.5 = (f32[3,1,16,128]{3,2,1,0:T(8,128)S(1)}, f32[3,1,16,128]{3,2,1,0:T(8,128)S(1)}, u32[]{:S(2)}, u32[]{:S(2)}) collective-permute-start(f32[3,1,16,128]{3,2,1,0:T(8,128)S(1)} %get-tuple-element.61), channel_id=1, source_target_pairs={{0,4},{4,8},{8,12},{12,16},{16,20},{20,24},{24,28},{1,5},{5,9},{9,... | collective-permute-start | bytes 73736 | tf_op jit(solution)/shard_map/ppermute | solution.py:20
  90.5 0.8 collective-permute-done.5
  91.4 1.3 collective-permute-start.6
  92.7 4.8 %collective-permute-start.7 = (f32[3,10,1,128]{3,2,1,0:T(1,128)S(1)}, f32[3,10,1,128]{3,2,1,0:T(1,128)S(1)}, u32[]{:S(2)}, u32[]{:S(2)}) collective-permute-start(f32[3,10,1,128]{3,2,1,0:T(1,128)S(1)} %get-tuple-element.56), channel_id=1, source_target_pairs={{0,1},{1,2},{2,3},{4,5},{5,6},{6,7},{8,9},{9,10},{10,11},{12,13},{... | collective-permute-start | bytes 46088 | tf_op jit(solution)/shard_map/ppermute | solution.py:20
  97.5 1.4 collective-permute-done.7
  99.8 1.3 collective-permute-start.8
  101.1 4.6 %collective-permute-start.9 = (f32[6,1,16,128]{3,2,1,0:T(8,128)S(1)}, f32[6,1,16,128]{3,2,1,0:T(8,128)S(1)}, u32[]{:S(2)}, u32[]{:S(2)}) collective-permute-start(f32[6,1,16,128]{3,2,1,0:T(8,128)S(1)} %get-tuple-element.48), channel_id=1, source_target_pairs={{0,4},{4,8},{8,12},{12,16},{16,20},{20,24},{24,28},{1,5},{5,9},{9,... | collective-permute-start | bytes 147464 | tf_op jit(solution)/shard_map/ppermute | solution.py:20
  105.7 0.8 collective-permute-done.9
  106.6 1.3 collective-permute-start.10
  107.9 4.7 %collective-permute-start.11 = (f32[6,10,1,128]{3,2,1,0:T(1,128)S(1)}, f32[6,10,1,128]{3,2,1,0:T(1,128)S(1)}, u32[]{:S(2)}, u32[]{:S(2)}) collective-permute-start(f32[6,10,1,128]{3,2,1,0:T(1,128)S(1)} %get-tuple-element.42), channel_id=1, source_target_pairs={{0,1},{1,2},{2,3},{4,5},{5,6},{6,7},{8,9},{9,10},{10,11},{12,13},{... | collective-permute-start | bytes 92168 | tf_op jit(solution)/shard_map/ppermute | solution.py:20
  112.8 9.9 %scatter_custom_fusion.3 = f32[3,16384]{0,1:T(8,128)} fusion(s32[1024]{0:T(1024)S(1)} %bitcast.215, f32[]{:T(128)} %constant.11.clone.1, f32[1,1024,3]{2,1,0:T(8,128)S(1)} %copy.114), kind=kCustom, calls=%fused_computation.11 | custom fusion | flops 3072 | bytes 720900 | tf_op jit(solution)/shard_map/scatter-add | solution.py:126
  122.8 5.2 %copy.109 = f32[3,8,16,128]{3,2,1,0:T(8,128)S(1)} copy(f32[3,8,16,128]{0,3,2,1:T(8,128)} %bitcast.187) | data formatting | bytes 393216 | tf_op jit(solution)/shard_map/reshape | solution.py:127
  128.0 0.7 select_maximum_fusion
  129.2 1.3 collective-permute-start.12
  130.5 6.2 %collective-permute-start.13 = (f32[3,1,16,128]{3,2,1,0:T(8,128)S(1)}, f32[3,1,16,128]{3,2,1,0:T(8,128)S(1)}, u32[]{:S(2)}, u32[]{:S(2)}) collective-permute-start(f32[3,1,16,128]{3,2,1,0:T(8,128)S(1)} %get-tuple-element.59), channel_id=1, source_target_pairs={{0,4},{4,8},{8,12},{12,16},{16,20},{20,24},{24,28},{1,5},{5,9},{9,... | collective-permute-start | bytes 73736 | tf_op jit(solution)/shard_map/ppermute | solution.py:20
  136.8 0.8 collective-permute-done.13
  137.6 1.3 collective-permute-start.14
  138.9 4.5 %collective-permute-start.15 = (f32[3,10,1,128]{3,2,1,0:T(1,128)S(1)}, f32[3,10,1,128]{3,2,1,0:T(1,128)S(1)}, u32[]{:S(2)}, u32[]{:S(2)}) collective-permute-start(f32[3,10,1,128]{3,2,1,0:T(1,128)S(1)} %get-tuple-element.52), channel_id=1, source_target_pairs={{0,1},{1,2},{2,3},{4,5},{5,6},{6,7},{8,9},{9,10},{10,11},{12,13},{... | collective-permute-start | bytes 46088 | tf_op jit(solution)/shard_map/ppermute | solution.py:20
  143.9 0.7 gather_fusion
  144.6 0.6 dynamic-slice
  145.2 0.6 stack.110
  145.8 5.3 %copy.111 = f32[6,16384]{0,1:T(8,128)} copy(f32[6,16384]{1,0:T(8,128)S(1)} %stack.110) | data formatting | bytes 786432 | tf_op jit(solution)/shard_map/stack | solution.py:47
  151.2 4.1 %gather_fusion.1 = f32[256,6]{1,0:T(8,128)S(1)} fusion(f32[6,16384]{0,1:T(8,128)} %copy.111, s32[1024]{0:T(1024)S(1)} %get-tuple-element.67), kind=kCustom, calls=%fused_computation.1 | custom fusion | bytes 13312 | tf_op jit(solution)/shard_map/gather | solution.py:132
  155.3 0.4 select_maximum_fusion.8
  156.1 0.6 stack.118
  156.7 5.3 %copy.112 = f32[6,16384]{0,1:T(8,128)} copy(f32[6,16384]{1,0:T(8,128)S(1)} %stack.118) | data formatting | bytes 786432 | tf_op jit(solution)/shard_map/stack | solution.py:47
  162.1 4.1 %gather_fusion.3 = f32[256,6]{1,0:T(8,128)S(1)} fusion(f32[6,16384]{0,1:T(8,128)} %copy.112, s32[1024]{0:T(1024)S(1)} %get-tuple-element.67), kind=kCustom, calls=%fused_computation.3 | custom fusion | bytes 13312 | tf_op jit(solution)/shard_map/gather | solution.py:132
  166.3 2.0 scatter_custom_fusion.4
  168.3 2.0 scatter_custom_fusion.5
  170.3 11.8 %gather_fusion.2 = f32[2048]{0:T(1024)S(1)} fusion(f32[2048]{0:T(1024)S(1)} %scatter_custom_fusion.4, s32[2048]{0:T(1024)S(1)} %fusion.56), kind=kCustom, calls=%fused_computation.2 | custom fusion | bytes 24576 | tf_op jit(solution)/shard_map/gather | solution.py:135
  182.1 11.8 %gather_fusion.4 = f32[2048]{0:T(1024)S(1)} fusion(f32[2048]{0:T(1024)S(1)} %scatter_custom_fusion.5, s32[2048]{0:T(1024)S(1)} %fusion.56), kind=kCustom, calls=%fused_computation.4 | custom fusion | bytes 24576 | tf_op jit(solution)/shard_map/gather | solution.py:135
  193.9 27.3 %all-reduce.4 = f32[2,8,256]{2,0,1:T(2,128)S(1)} all-reduce(f32[2,8,256]{2,0,1:T(2,128)S(1)} %pad_maximum_fusion.38), channel_id=2, replica_groups=mesh['strike'=8,'dip'=4] {'strike'}, use_global_device_ids=true, to_apply=%region_9.10.clone | all-reduce | flops 4096 | bytes 32768
  221.2 0.6 constant_dynamic-slice_fusion
  221.8 0.8 copy.115
  222.6 21.3 %reduce-scatter.4.cloned.1.call-done = f32[64,2]{1,0:T(8,128)} async-done(((f32[256,2]{1,0:T(8,128)}), f32[64,2]{1,0:T(8,128)}) %reduce-scatter.4.cloned.1.call-update) | async-done | bytes 528
  244.0 1.4 copy.116
  (92 shorter events, 4.3 us)
Async XLA Ops:
  7.2 62.6 %copy-start = (f32[2,128]{1,0:T(2,128)S(1)}, f32[2,128]{1,0:T(2,128)}, u32[]{:S(2)}) copy-start(f32[2,128]{1,0:T(2,128)} %param.20) | copy-start | bytes 3076
  12.2 9.9 %all-to-all-start = ((s32[8,1,128]{2,1,0:T(1,128)}), s32[8,1,128]{2,1,0:T(1,128)S(1)}, u32[]{:S(2)}, u32[]{:S(2)}) async-start(s32[8,1,128]{2,1,0:T(1,128)} %reshape.266), calls=%async_computation | async-start | bytes 8192 | tf_op jit(solution)/shard_map/all_to_all | solution.py:108
  22.2 16.8 %all-to-all-start.2 = ((bf16[8,4,32,384]{3,2,1,0:T(8,128)(2,1)}), bf16[8,4,32,384]{3,2,1,0:T(8,128)(2,1)S(1)}, u32[]{:S(2)}, u32[]{:S(2)}) async-start(bf16[8,4,32,384]{3,2,1,0:T(8,128)(2,1)} %bitcast.5), calls=%async_computation.2 | async-start | bytes 1572864 | tf_op jit(solution)/shard_map/all_to_all | solution.py:101
  38.9 10.5 %all-to-all-start.1 = ((s32[4,1,256]{2,1,0:T(1,128)}), s32[4,1,256]{2,1,0:T(1,128)S(1)}, u32[]{:S(2)}, u32[]{:S(2)}) async-start(s32[4,1,256]{2,1,0:T(1,128)} %reshape.268), calls=%async_computation.1 | async-start | bytes 8192 | tf_op jit(solution)/shard_map/all_to_all | solution.py:107
  43.8 9.1 %copy-start.2 = (f32[9,8,16,128]{3,2,1,0:T(8,128)S(1)}, f32[9,8,16,128]{3,2,1,0:T(8,128)}, u32[]{:S(2)}) copy-start(f32[9,8,16,128]{3,2,1,0:T(8,128)} %param.13) | copy-start | bytes 1769476
  49.4 20.0 %all-to-all-start.3 = ((bf16[8,4,32,384]{3,2,0,1:T(8,128)(2,1)}), bf16[8,4,32,384]{3,2,0,1:T(8,128)(2,1)S(1)}, u32[]{:S(2)}, u32[]{:S(2)}) async-start(bf16[8,4,32,384]{3,2,0,1:T(8,128)(2,1)} %copy.103), calls=%async_computation.3 | async-start | bytes 1572864 | tf_op jit(solution)/shard_map/all_to_all | solution.py:100
  52.9 191.1 %reduce-scatter.4.cloned.1.call-start = ((), (), s32[]{:S(2)}) async-start(), calls=%async_computation.5 | async-start | bytes 163840
  53.0 5.2 %collective-permute-start = (f32[6,1,16,128]{3,2,1,0:T(8,128)S(1)}, f32[6,1,16,128]{3,2,1,0:T(8,128)S(1)}, u32[]{:S(2)}, u32[]{:S(2)}) collective-permute-start(f32[6,1,16,128]{3,2,1,0:T(8,128)S(1)} %get-tuple-element.39), channel_id=1, source_target_pairs={{4,0},{8,4},{12,8},{16,12},{20,16},{24,20},{28,24},{5,1},{9,5},{13... | collective-permute-start | bytes 147464 | tf_op jit(solution)/shard_map/ppermute | solution.py:22
  54.3 3.9 %collective-permute-start.1 = (f32[6,1,16,128]{3,2,1,0:T(8,128)S(1)}, f32[6,1,16,128]{3,2,1,0:T(8,128)S(1)}, u32[]{:S(2)}, u32[]{:S(2)}) collective-permute-start(f32[6,1,16,128]{3,2,1,0:T(8,128)S(1)} %get-tuple-element.38), channel_id=1, source_target_pairs={{0,4},{4,8},{8,12},{12,16},{16,20},{20,24},{24,28},{1,5},{5,9},{9,... | collective-permute-start | bytes 147464 | tf_op jit(solution)/shard_map/ppermute | solution.py:20
  58.2 6.0 %collective-permute-start.2 = (f32[6,10,1,128]{3,2,1,0:T(1,128)S(1)}, f32[6,10,1,128]{3,2,1,0:T(1,128)S(1)}, u32[]{:S(2)}, u32[]{:S(2)}) collective-permute-start(f32[6,10,1,128]{3,2,1,0:T(1,128)S(1)} %get-tuple-element.47), channel_id=1, source_target_pairs={{1,0},{2,1},{3,2},{5,4},{6,5},{7,6},{9,8},{10,9},{11,10},{13,12},{... | collective-permute-start | bytes 92168 | tf_op jit(solution)/shard_map/ppermute | solution.py:22
  59.5 6.1 %collective-permute-start.3 = (f32[6,10,1,128]{3,2,1,0:T(1,128)S(1)}, f32[6,10,1,128]{3,2,1,0:T(1,128)S(1)}, u32[]{:S(2)}, u32[]{:S(2)}) collective-permute-start(f32[6,10,1,128]{3,2,1,0:T(1,128)S(1)} %get-tuple-element.46), channel_id=1, source_target_pairs={{0,1},{1,2},{2,3},{4,5},{5,6},{6,7},{8,9},{9,10},{10,11},{12,13},{... | collective-permute-start | bytes 92168 | tf_op jit(solution)/shard_map/ppermute | solution.py:20
  80.7 5.3 %copy-start.4 = (f32[8,16,128]{2,1,0:T(8,128)S(1)}, f32[8,16,128]{2,1,0:T(8,128)}, u32[]{:S(2)}) copy-start(f32[8,16,128]{2,1,0:T(8,128)} %param.16) | copy-start | bytes 196612
  86.0 13.5 %copy-start.1 = (f32[8,16,128]{2,1,0:T(8,128)S(1)}, f32[8,16,128]{2,1,0:T(8,128)}, u32[]{:S(2)}) copy-start(f32[8,16,128]{2,1,0:T(8,128)} %param.15) | copy-start | bytes 196612
  86.0 13.5 %copy-start.3 = (f32[8,16,128]{2,1,0:T(8,128)S(1)}, f32[8,16,128]{2,1,0:T(8,128)}, u32[]{:S(2)}) copy-start(f32[8,16,128]{2,1,0:T(8,128)} %param.14) | copy-start | bytes 196612
  86.0 4.5 %collective-permute-start.4 = (f32[3,1,16,128]{3,2,1,0:T(8,128)S(1)}, f32[3,1,16,128]{3,2,1,0:T(8,128)S(1)}, u32[]{:S(2)}, u32[]{:S(2)}) collective-permute-start(f32[3,1,16,128]{3,2,1,0:T(8,128)S(1)} %get-tuple-element.60), channel_id=1, source_target_pairs={{4,0},{8,4},{12,8},{16,12},{20,16},{24,20},{28,24},{5,1},{9,5},{13... | collective-permute-start | bytes 73736 | tf_op jit(solution)/shard_map/ppermute | solution.py:22
  87.5 3.9 %collective-permute-start.5 = (f32[3,1,16,128]{3,2,1,0:T(8,128)S(1)}, f32[3,1,16,128]{3,2,1,0:T(8,128)S(1)}, u32[]{:S(2)}, u32[]{:S(2)}) collective-permute-start(f32[3,1,16,128]{3,2,1,0:T(8,128)S(1)} %get-tuple-element.61), channel_id=1, source_target_pairs={{0,4},{4,8},{8,12},{12,16},{16,20},{20,24},{24,28},{1,5},{5,9},{9,... | collective-permute-start | bytes 73736 | tf_op jit(solution)/shard_map/ppermute | solution.py:20
  91.4 6.1 %collective-permute-start.6 = (f32[3,10,1,128]{3,2,1,0:T(1,128)S(1)}, f32[3,10,1,128]{3,2,1,0:T(1,128)S(1)}, u32[]{:S(2)}, u32[]{:S(2)}) collective-permute-start(f32[3,10,1,128]{3,2,1,0:T(1,128)S(1)} %get-tuple-element.57), channel_id=1, source_target_pairs={{1,0},{2,1},{3,2},{5,4},{6,5},{7,6},{9,8},{10,9},{11,10},{13,12},{... | collective-permute-start | bytes 46088 | tf_op jit(solution)/shard_map/ppermute | solution.py:22
  92.7 6.2 %collective-permute-start.7 = (f32[3,10,1,128]{3,2,1,0:T(1,128)S(1)}, f32[3,10,1,128]{3,2,1,0:T(1,128)S(1)}, u32[]{:S(2)}, u32[]{:S(2)}) collective-permute-start(f32[3,10,1,128]{3,2,1,0:T(1,128)S(1)} %get-tuple-element.56), channel_id=1, source_target_pairs={{0,1},{1,2},{2,3},{4,5},{5,6},{6,7},{8,9},{9,10},{10,11},{12,13},{... | collective-permute-start | bytes 46088 | tf_op jit(solution)/shard_map/ppermute | solution.py:20
  99.5 6.1 %copy-start.7 = (s32[2048]{0:T(1024)S(1)}, s32[2048]{0:T(1024)}, u32[]{:S(2)}) copy-start(s32[2048]{0:T(1024)} %param.25) | copy-start | bytes 24580
  99.6 13.0 %copy-start.9 = (s32[1,256]{1,0:T(1,128)S(1)}, s32[1,256]{1,0:T(1,128)}, u32[]{:S(2)}) copy-start(s32[1,256]{1,0:T(1,128)} %param.21) | copy-start | bytes 3076
  99.8 5.9 %collective-permute-start.8 = (f32[6,1,16,128]{3,2,1,0:T(8,128)S(1)}, f32[6,1,16,128]{3,2,1,0:T(8,128)S(1)}, u32[]{:S(2)}, u32[]{:S(2)}) collective-permute-start(f32[6,1,16,128]{3,2,1,0:T(8,128)S(1)} %get-tuple-element.49), channel_id=1, source_target_pairs={{4,0},{8,4},{12,8},{16,12},{20,16},{24,20},{28,24},{5,1},{9,5},{13... | collective-permute-start | bytes 147464 | tf_op jit(solution)/shard_map/ppermute | solution.py:22
  101.1 5.4 %collective-permute-start.9 = (f32[6,1,16,128]{3,2,1,0:T(8,128)S(1)}, f32[6,1,16,128]{3,2,1,0:T(8,128)S(1)}, u32[]{:S(2)}, u32[]{:S(2)}) collective-permute-start(f32[6,1,16,128]{3,2,1,0:T(8,128)S(1)} %get-tuple-element.48), channel_id=1, source_target_pairs={{0,4},{4,8},{8,12},{12,16},{16,20},{20,24},{24,28},{1,5},{5,9},{9,... | collective-permute-start | bytes 147464 | tf_op jit(solution)/shard_map/ppermute | solution.py:20
  106.6 21.5 %collective-permute-start.10 = (f32[6,10,1,128]{3,2,1,0:T(1,128)S(1)}, f32[6,10,1,128]{3,2,1,0:T(1,128)S(1)}, u32[]{:S(2)}, u32[]{:S(2)}) collective-permute-start(f32[6,10,1,128]{3,2,1,0:T(1,128)S(1)} %get-tuple-element.43), channel_id=1, source_target_pairs={{1,0},{2,1},{3,2},{5,4},{6,5},{7,6},{9,8},{10,9},{11,10},{13,12},{... | collective-permute-start | bytes 92168 | tf_op jit(solution)/shard_map/ppermute | solution.py:22
  107.9 20.2 %collective-permute-start.11 = (f32[6,10,1,128]{3,2,1,0:T(1,128)S(1)}, f32[6,10,1,128]{3,2,1,0:T(1,128)S(1)}, u32[]{:S(2)}, u32[]{:S(2)}) collective-permute-start(f32[6,10,1,128]{3,2,1,0:T(1,128)S(1)} %get-tuple-element.42), channel_id=1, source_target_pairs={{0,1},{1,2},{2,3},{4,5},{5,6},{6,7},{8,9},{9,10},{10,11},{12,13},{... | collective-permute-start | bytes 92168 | tf_op jit(solution)/shard_map/ppermute | solution.py:20
  128.9 7.8 %copy-start.10 = (s32[1,256]{1,0:T(1,128)S(1)}, s32[1,256]{1,0:T(1,128)}, u32[]{:S(2)}) copy-start(s32[1,256]{1,0:T(1,128)} %param.22) | copy-start | bytes 3076
  128.9 14.5 %copy-start.6 = (f32[6,2048]{1,0:T(8,128)S(1)}, f32[6,2048]{1,0:T(8,128)}, u32[]{:S(2)}) copy-start(f32[6,2048]{1,0:T(8,128)} %param.24) | copy-start | bytes 147460
  129.2 15.4 %copy-start.11 = (u32[32]{0:T(128)S(1)}, u32[32]{0:T(128)}, u32[]{:S(2)}) copy-start(u32[32]{0:T(128)} %constant.44) | copy-start | bytes 388
  129.2 7.5 %collective-permute-start.12 = (f32[3,1,16,128]{3,2,1,0:T(8,128)S(1)}, f32[3,1,16,128]{3,2,1,0:T(8,128)S(1)}, u32[]{:S(2)}, u32[]{:S(2)}) collective-permute-start(f32[3,1,16,128]{3,2,1,0:T(8,128)S(1)} %get-tuple-element.58), channel_id=1, source_target_pairs={{4,0},{8,4},{12,8},{16,12},{20,16},{24,20},{28,24},{5,1},{9,5},{13... | collective-permute-start | bytes 73736 | tf_op jit(solution)/shard_map/ppermute | solution.py:22
  130.5 7.0 %collective-permute-start.13 = (f32[3,1,16,128]{3,2,1,0:T(8,128)S(1)}, f32[3,1,16,128]{3,2,1,0:T(8,128)S(1)}, u32[]{:S(2)}, u32[]{:S(2)}) collective-permute-start(f32[3,1,16,128]{3,2,1,0:T(8,128)S(1)} %get-tuple-element.59), channel_id=1, source_target_pairs={{0,4},{4,8},{8,12},{12,16},{16,20},{20,24},{24,28},{1,5},{5,9},{9,... | collective-permute-start | bytes 73736 | tf_op jit(solution)/shard_map/ppermute | solution.py:20
  137.6 17.7 %collective-permute-start.14 = (f32[3,10,1,128]{3,2,1,0:T(1,128)S(1)}, f32[3,10,1,128]{3,2,1,0:T(1,128)S(1)}, u32[]{:S(2)}, u32[]{:S(2)}) collective-permute-start(f32[3,10,1,128]{3,2,1,0:T(1,128)S(1)} %get-tuple-element.53), channel_id=1, source_target_pairs={{1,0},{2,1},{3,2},{5,4},{6,5},{7,6},{9,8},{10,9},{11,10},{13,12},{... | collective-permute-start | bytes 46088 | tf_op jit(solution)/shard_map/ppermute | solution.py:22
  138.9 16.4 %collective-permute-start.15 = (f32[3,10,1,128]{3,2,1,0:T(1,128)S(1)}, f32[3,10,1,128]{3,2,1,0:T(1,128)S(1)}, u32[]{:S(2)}, u32[]{:S(2)}) collective-permute-start(f32[3,10,1,128]{3,2,1,0:T(1,128)S(1)} %get-tuple-element.52), channel_id=1, source_target_pairs={{0,1},{1,2},{2,3},{4,5},{5,6},{6,7},{8,9},{9,10},{10,11},{12,13},{... | collective-permute-start | bytes 46088 | tf_op jit(solution)/shard_map/ppermute | solution.py:20
  156.1 6.0 %copy-start.5 = (f32[9,8,16,128]{3,2,1,0:T(8,128)}, f32[9,8,16,128]{3,2,1,0:T(8,128)S(1)}, u32[]{:S(2)}) copy-start(f32[9,8,16,128]{3,2,1,0:T(8,128)S(1)} %get-tuple-element.4) | copy-start | bytes 1769476
  156.7 9.6 %copy-start.8 = (f32[1,256]{1,0:T(1,128)S(1)}, f32[1,256]{1,0:T(1,128)}, u32[]{:S(2)}) copy-start(f32[1,256]{1,0:T(1,128)} %param.23) | copy-start | bytes 3076
Sparse Core Ops, SparseCore 0:
  222.8 21.1 reduce-scatter.3
where the time goes:
time: 254 us; the launch traced here: 252 us
  local copies, waits for them, and re-layouts  70.2 us (28%)
  starting transfers between devices  63.8 us (25%)
  waiting for transfers between devices  44.6 us (18%)
  other arithmetic  30.9 us (12%)
  blocking collectives  27.3 us (11%)
  between operations  14.8 us (6%)
    ppermute x8, starting transfers between devices, with_halo(): lax.ppermute(tail, axis, [(i, (i + 1) % count) for i in range(ends)])  35.5 us
    unnamed x1, blocking collectives  27.3 us
    gather x2, local copies, waits for them, and re-layouts, shards(): partials.append(partial_sum[subpatch_order])  23.6 us
    unnamed x2, waiting for transfers between devices  21.4 us
    scatter-add x2, other arithmetic, shards(): jnp.zeros((3, cell_total), jnp.float32).at[:, arrived_cells]  19.9 us
    another operation x4, local copies, waits for them, and re-layouts, stress_update(): jnp.stack([stress[0] + time_step * (lame_lambda * dilation + 2.0 * lame_m...  11.9 us
    all_to_all x1, waiting for transfers between devices, shards(): lax.all_to_all(outgoing, 'strike', split_axis=0, concat_axis=0, tiled=True)  10.6 us
    reshape x2, local copies, waits for them, and re-layouts, shards(): source = source.reshape(3, local_x, local_y, local_z)  10.5 us
  transfers between devices with their start and end apart: 21, of which 10 were waited for; matrix products, arithmetic and copies ran while one was open for 15% of the time, Pallas kernels for 0%

commit v1 on v0

v1 whole, which is shorter than its diff:
```python
import functools

import jax
import jax.numpy as jnp
from jax import lax
from jax.experimental import pallas as pl
from jax.experimental.pallas import tpu as pltpu
from jax.sharding import PartitionSpec as P

STEPS = 2
LANES = 128

time_step = 0.25

MESH = pl.DeviceIdType.MESH
NT_DIMS = (((1,), (1,)), ((), ()))


def split(x):
    high = x.astype(jnp.bfloat16)
    return high, (x - high.astype(jnp.float32)).astype(jnp.bfloat16)


def one_hot(shape, axis, ids):
    return jnp.where(lax.broadcasted_iota(jnp.int32, shape, axis) == ids, 1.0, 0.0).astype(jnp.bfloat16)


def matmul(a, b):
    return jnp.dot(a, b, preferred_element_type=jnp.float32)


def matmul_nt(a, b):
    return lax.dot_general(a, b, NT_DIMS, preferred_element_type=jnp.float32)


def along_x(f, low, high):
    before = jnp.concatenate([low[None], f[:-1]], axis=0)
    after = jnp.concatenate([f[1:], high[None]], axis=0)
    return (after - before) * 0.5


def along_y(f, low, high):
    size = f.shape[1]
    at = lax.broadcasted_iota(jnp.int32, f.shape, 1)
    before = jnp.where(at == 0, low, pltpu.roll(f, 1, 1))
    after = jnp.where(at == size - 1, high, pltpu.roll(f, size - 1, 1))
    return (after - before) * 0.5


def along_z(f):
    size = f.shape[2]
    at = lax.broadcasted_iota(jnp.int32, f.shape, 2)
    before = jnp.where(at == 0, 0.0, pltpu.roll(f, 1, 2))
    after = jnp.where(at == size - 1, 0.0, pltpu.roll(f, size - 1, 2))
    return (after - before) * 0.5


def kernel(
    strike_count,
    dip_count,
    slot_count,
    state,
    lam,
    mu,
    buoy,
    residual,
    tiles,
    cells,
    resample,
    patch,
    fault_cell,
    area,
    moment,
    order,
    out,
    slip,
    packed,
    landed,
    source,
    onehot_hi,
    picks,
    sums_out,
    sums_in,
    x_out,
    x_low,
    x_high,
    y_out,
    y_low,
    y_high,
    route_send,
    route_recv,
    sum_send,
    sum_recv,
    halo_send,
    halo_recv,
):
    count = strike_count * dip_count
    strike = lax.axis_index("strike")
    dip = lax.axis_index("dip")
    me = strike * dip_count + dip
    size_x, size_y, size_z = buoy.shape
    rows = size_x * size_y
    stations = residual.shape[1]
    steps = resample.shape[0]
    shift = size_z.bit_length() - 1
    slots = count * slot_count
    groups = slots // LANES
    per_group = LANES // slot_count
    owned = order.shape[1] // count
    per_block = LANES // owned
    blocks = order.shape[1] // LANES

    def peer(k):
        to = lax.rem(me + k, count)
        return to, (to // dip_count, lax.rem(to, dip_count))

    barrier = pltpu.get_barrier_semaphore()

    def greet(k, carry):
        _, device = peer(k)
        pl.semaphore_signal(barrier, inc=1, device_id=device, device_id_type=MESH)
        return carry

    lax.fori_loop(1, count, greet, 0)

    sides = (
        (strike > 0, (strike - 1, dip)),
        (strike < strike_count - 1, (strike + 1, dip)),
        (dip > 0, (strike, dip - 1)),
        (dip < dip_count - 1, (strike, dip + 1)),
    )
    halves = ((x_out, x_low, x_high), (y_out, y_low, y_high))

    def halo_copies(turn):
        copies = []
        for side in range(4):
            sender, low, high = halves[side // 2]
            target = high if side % 2 == 0 else low
            arrival = side ^ 1
            copies.append(
                pltpu.make_async_remote_copy(
                    src_ref=sender.at[turn, side % 2],
                    dst_ref=target.at[turn],
                    send_sem=halo_send.at[turn, side],
                    recv_sem=halo_recv.at[turn, arrival],
                    device_id=sides[side][1],
                    device_id_type=MESH,
                )
            )
        return copies

    def stage(turn, x_fields, y_fields):
        for c in range(3):
            f = out[x_fields[c]] if turn else state[x_fields[c]]
            x_out[turn, 0, c] = f[0]
            x_out[turn, 1, c] = f[size_x - 1]
            f = out[y_fields[c]] if turn else state[y_fields[c]]
            y_out[turn, 0, c] = f[:, 0:1]
            y_out[turn, 1, c] = f[:, size_y - 1 : size_y]

    def send(turn):
        for side, copy in enumerate(halo_copies(turn)):
            pl.when(sides[side][0])(copy.start)

    def receive(turn):
        for side, copy in enumerate(halo_copies(turn)):

            def finish(turn=turn, side=side, copy=copy):
                copy.wait_send()
                sender, low, high = halves[side // 2]
                target = low if side % 2 == 0 else high
                pltpu.make_async_copy(target.at[turn], target.at[turn], halo_recv.at[turn, side]).wait()

            pl.when(sides[side][0])(finish)

    for side in range(4):

        def clear(side=side):
            _, low, high = halves[side // 2]
            target = low if side % 2 == 0 else high
            target[...] = jnp.zeros_like(target)

        pl.when(jnp.logical_not(sides[side][0]))(clear)

    stress_x, stress_y = (3, 6, 7), (6, 4, 8)
    stage(0, stress_x, stress_y)

    res_hi, res_lo = split(resample[...])
    weights = jnp.concatenate([res_hi, res_lo], axis=0)
    parts = [matmul_nt(weights, residual[c]) for c in range(3)]
    amplitude = [parts[c][k : k + 1] + parts[c][steps + k : steps + k + 1] for k in range(steps) for c in range(3)]
    cell_row = cells[...]
    hi_row = lax.shift_right_logical(cell_row, shift).astype(jnp.float32)
    lo_row = (cell_row & (size_z - 1)).astype(jnp.float32)
    values = jnp.concatenate(amplitude + [hi_row, lo_row], axis=0)
    tile_row = tiles[...]
    named = one_hot((count, stations), 0, tile_row)
    earlier = jnp.where(
        lax.broadcasted_iota(jnp.int32, (stations, stations), 0) < lax.broadcasted_iota(jnp.int32, (stations, stations), 1),
        1.0,
        0.0,
    ).astype(jnp.bfloat16)
    ordinal = jnp.sum(named.astype(jnp.float32) * matmul(named, earlier), axis=0, keepdims=True)
    slot_row = tile_row * slot_count + ordinal.astype(jnp.int32)
    placing = one_hot((slots, stations), 0, slot_row)
    val_hi, val_lo = split(values)
    placed = matmul_nt(jnp.concatenate([val_hi, val_lo], axis=0), placing)
    placed = placed[:8] + placed[8:]
    for g in range(groups):
        packed[g] = placed[:, g * LANES : (g + 1) * LANES]

    pl.semaphore_wait(barrier, count - 1)
    send(0)

    def route(k, carry):
        to, device = peer(k)
        pltpu.make_async_remote_copy(
            src_ref=packed.at[to // per_group],
            dst_ref=landed.at[me],
            send_sem=route_send,
            recv_sem=route_recv,
            device_id=device,
            device_id_type=MESH,
        ).start()
        return carry

    lax.fori_loop(1, count, route, 0)
    landed[me] = packed[me // per_group]

    patch_row = patch[...]
    entries = patch_row.shape[1]
    cell_e = fault_cell[...]
    pick_lo = one_hot((size_z, entries), 0, cell_e & (size_z - 1))
    onehot_hi[...] = jnp.where(
        lax.broadcasted_iota(jnp.int32, (rows, entries), 0) == lax.shift_right_logical(cell_e, shift), 1.0, 0.0
    )
    mom_hi, mom_lo = split(moment[...])
    chosen = matmul(jnp.concatenate([mom_hi, mom_lo], axis=0), one_hot((moment.shape[1], entries), 0, patch_row))
    pattern = (chosen[:6] + chosen[6:]) * area[...]
    patch_col = jnp.transpose(jnp.broadcast_to(patch_row.astype(jnp.float32), (LANES, entries)))
    for b in range(blocks):
        ids = order[:, b * LANES : (b + 1) * LANES].astype(jnp.float32)
        picks[:, b * LANES : (b + 1) * LANES] = jnp.where(patch_col == ids, 1.0, 0.0).astype(jnp.bfloat16)

    def force(turn, c, fields):
        xx, yy, zz = fields
        fx = (out if turn else state)[xx]
        fy = (out if turn else state)[yy]
        fz = (out if turn else state)[zz]
        total = along_x(fx, x_low[turn, c], x_high[turn, c]) + along_y(fy, y_low[turn, c], y_high[turn, c]) + along_z(fz)
        return time_step * (buoy[...] * total)

    rhs = ((3, 6, 7), (6, 4, 8), (7, 8, 5))

    def velocity(turn, step):
        for c in range(3):
            old = (out if turn else state)[c]
            moved = old + force(turn, c, rhs[c])
            if step:
                moved = moved + time_step * source[step * 3 + c].reshape(size_x, size_y, size_z)
            out[c] = moved

    def stress(turn, first):
        old = state if first else out
        lam_v, mu_v = lam[...], mu[...]
        vx, vy, vz = out[0], out[1], out[2]
        dxx = along_x(vx, x_low[turn, 0], x_high[turn, 0])
        dyy = along_y(vy, y_low[turn, 1], y_high[turn, 1])
        dzz = along_z(vz)
        bulk = lam_v * (dxx + dyy + dzz)
        out[3] = old[3] + time_step * (bulk + 2.0 * mu_v * dxx)
        out[4] = old[4] + time_step * (bulk + 2.0 * mu_v * dyy)
        out[5] = old[5] + time_step * (bulk + 2.0 * mu_v * dzz)
        scaled = time_step * mu_v
        out[6] = old[6] + scaled * (
            along_y(vx, y_low[turn, 0], y_high[turn, 0]) + along_x(vy, x_low[turn, 1], x_high[turn, 1])
        )
        out[7] = old[7] + scaled * (along_z(vx) + along_x(vz, x_low[turn, 2], x_high[turn, 2]))
        out[8] = old[8] + scaled * (along_z(vy) + along_y(vz, y_low[turn, 2], y_high[turn, 2]))

    def contribution():
        total = None
        for m in range(6):
            high, low = split(out[3 + m].reshape(rows, size_z))
            taken = (matmul(high, pick_lo) + matmul(low, pick_lo)) * pattern[m : m + 1]
            total = taken if total is None else total + taken
        return jnp.sum(total * onehot_hi[...], axis=0, keepdims=True)

    receive(0)
    velocity(0, 0)

    all_landed = landed.at[pl.ds(0, count - 1)]
    pltpu.make_async_copy(all_landed, all_landed, route_recv).wait()
    pltpu.make_async_copy(all_landed, all_landed, route_send).wait()
    mine = lax.rem(me, per_group)
    lane = lax.broadcasted_iota(jnp.int32, (8, LANES), 1)
    gathered = []
    for g in range(groups):
        total = jnp.zeros((8, LANES), jnp.float32)
        for j in range(per_group):
            turned = pltpu.roll(landed[g * per_group + j], lax.rem(j - mine + per_group, per_group) * slot_count, 1)
            total = jnp.where(lane // slot_count == j, turned, total)
        gathered.append(total)
    arrived = jnp.concatenate(gathered, axis=1)
    hi_ids = arrived[6:7].astype(jnp.int32)
    lo_ids = arrived[7:8].astype(jnp.int32)
    spread_lo = one_hot((size_z, slots), 0, lo_ids)
    row_mask = lax.broadcasted_iota(jnp.int32, (rows, slots), 0) == hi_ids
    amp_hi, amp_lo = split(arrived)
    amp_hi, amp_lo = amp_hi.astype(jnp.float32), amp_lo.astype(jnp.float32)
    for m in range(steps * 3):
        high = jnp.where(row_mask, amp_hi[m : m + 1], 0.0).astype(jnp.bfloat16)
        low = jnp.where(row_mask, amp_lo[m : m + 1], 0.0).astype(jnp.bfloat16)
        source[m] = matmul_nt(high, spread_lo) + matmul_nt(low, spread_lo)
    for c in range(3):
        out[c] = out[c] + time_step * source[c].reshape(size_x, size_y, size_z)

    flow = (0, 1, 2)
    contribs = []
    for step in range(steps):
        if step:
            receive(2 * step)
            velocity(2 * step, step)
        stage(2 * step + 1, flow, flow)
        send(2 * step + 1)
        receive(2 * step + 1)
        stress(2 * step + 1, step == 0)
        if step < steps - 1:
            stage(2 * step + 2, stress_x, stress_y)
            send(2 * step + 2)
        contribs.append(contribution())

    con_hi, con_lo = split(jnp.concatenate(contribs, axis=0))
    summed = matmul(jnp.concatenate([con_hi, con_lo], axis=0), picks[...])
    summed = summed[:steps] + summed[steps:]
    for b in range(blocks):
        sums_out[b] = summed[:, b * LANES : (b + 1) * LANES]

    def spread(k, carry):
        to, device = peer(k)
        pltpu.make_async_remote_copy(
            src_ref=sums_out.at[to // per_block],
            dst_ref=sums_in.at[me],
            send_sem=sum_send,
            recv_sem=sum_recv,
            device_id=device,
            device_id_type=MESH,
        ).start()
        return carry

    lax.fori_loop(1, count, spread, 0)
    sums_in[me] = sums_out[me // per_block]
    all_sums = sums_in.at[pl.ds(0, count - 1)]
    pltpu.make_async_copy(all_sums, all_sums, sum_recv).wait()
    pltpu.make_async_copy(all_sums, all_sums, sum_send).wait()
    final = jnp.sum(sums_in[...], axis=0)
    final = jnp.concatenate([final, jnp.zeros((8 - steps, LANES), jnp.float32)], axis=0)
    first = lax.rem(me, per_block) * owned
    slip[...] = pltpu.roll(final, lax.rem(LANES - first, LANES), 1)[:steps, :owned]


def shards(
    adjoint_state,
    lame_lambda,
    lame_mu,
    buoyancy,
    residual,
    receiver_tile,
    receiver_cell,
    resample,
    fault_patch,
    fault_cell,
    fault_area,
    moment,
    subpatch_order,
):
    strike_count = lax.axis_size("strike")
    dip_count = lax.axis_size("dip")
    count = strike_count * dip_count
    stations = residual.shape[0]
    slot_count = max(2, (2 * stations + count - 1) // count)
    steps = resample.shape[0]
    size_x, size_y, size_z = buoyancy.shape
    rows = size_x * size_y
    slots = count * slot_count
    entries = fault_patch.shape[1]
    patches = moment.shape[1]
    turns = 2 * steps
    vmem = pl.BlockSpec(memory_space=pltpu.VMEM)
    f32, bf16 = jnp.float32, jnp.bfloat16
    return pl.pallas_call(
        functools.partial(kernel, strike_count, dip_count, slot_count),
        out_shape=(
            jax.ShapeDtypeStruct(adjoint_state.shape, f32),
            jax.ShapeDtypeStruct((steps, patches // count), f32),
        ),
        in_specs=[vmem] * 13,
        out_specs=(vmem, vmem),
        scratch_shapes=[
            pltpu.VMEM((slots // LANES, 8, LANES), f32),
            pltpu.VMEM((count, 8, LANES), f32),
            pltpu.VMEM((steps * 3, rows, size_z), f32),
            pltpu.VMEM((rows, entries), f32),
            pltpu.VMEM((entries, patches), bf16),
            pltpu.VMEM((patches // LANES, steps, LANES), f32),
            pltpu.VMEM((count, steps, LANES), f32),
            pltpu.VMEM((turns, 2, 3, size_y, size_z), f32),
            pltpu.VMEM((turns, 3, size_y, size_z), f32),
            pltpu.VMEM((turns, 3, size_y, size_z), f32),
            pltpu.VMEM((turns, 2, 3, size_x, 1, size_z), f32),
            pltpu.VMEM((turns, 3, size_x, 1, size_z), f32),
            pltpu.VMEM((turns, 3, size_x, 1, size_z), f32),
            pltpu.SemaphoreType.DMA,
            pltpu.SemaphoreType.DMA,
            pltpu.SemaphoreType.DMA,
            pltpu.SemaphoreType.DMA,
            pltpu.SemaphoreType.DMA((turns, 4)),
            pltpu.SemaphoreType.DMA((turns, 4)),
        ],
        compiler_params=pltpu.CompilerParams(collective_id=0, has_side_effects=True),
        name="adjoint",
    )(
        adjoint_state,
        lame_lambda,
        lame_mu,
        buoyancy,
        jnp.swapaxes(residual, 0, 1),
        receiver_tile.reshape(1, stations),
        receiver_cell.reshape(1, stations),
        resample,
        fault_patch,
        fault_cell,
        fault_area,
        moment,
        subpatch_order.reshape(1, -1),
    )


def solution(mesh):
    return jax.shard_map(
        shards,
        mesh=mesh,
        in_specs=(
            P(None, "strike", "dip", None),
            P("strike", "dip", None),
            P("strike", "dip", None),
            P("strike", "dip", None),
            P(("strike", "dip"), None, None),
            P(("strike", "dip"), None),
            P(("strike", "dip")),
            P(),
            P(("strike", "dip"), None),
            P(("strike", "dip"), None),
            P(("strike", "dip"), None),
            P(),
            P(),
        ),
        out_specs=(P(None, "strike", "dip", None), P(None, ("strike", "dip"))),
        check_vma=False,
    )
```

time: 254 us -> 33.3 us (0.13)
  local copies, waits for them, and re-layouts: 70.2 us -> 2.48 us
  starting transfers between devices: 63.8 us -> 0 us
  waiting for transfers between devices: 44.6 us -> 0 us
  other arithmetic: 30.9 us -> 0 us
  Pallas kernels: 0 us -> 30 us
  blocking collectives: 27.3 us -> 0 us
  between operations: 14.8 us -> 0.65 us
    ppermute x16 -> x0, starting transfers between devices: 46 us -> none  [the longest x8 35.5 us: with_halo(): lax.ppermute(tail, axis, [(i, (i + 1) % count) for i in range(ends)])]
    gather x5 -> x0, local copies, waits for them, and re-layouts: 32.5 us -> none  [the longest x2 23.6 us: shards(): partials.append(partial_sum[subpatch_order])]
    pallas_call x0 -> x1, Pallas kernels: none -> 30 us  [shards(): pl.pallas_call(functools.partial(kernel, strike_count, dip_count, slot_co...]
    unnamed x1 -> x0, blocking collectives: 27.3 us -> none
    scatter-add x4 -> x0, other arithmetic: 23.8 us -> none  [the longest x2 19.9 us: shards(): jnp.zeros((3, cell_total), jnp.float32).at[:, arrived_cells]]
    unnamed x2 -> x0, waiting for transfers between devices: 21.4 us -> none
    all_to_all x4 -> x0, waiting for transfers between devices: 17.8 us -> none  [the longest x1 10.6 us: shards(): lax.all_to_all(outgoing, 'strike', split_axis=0, concat_axis=0, tiled=True)]
    all_to_all x4 -> x0, starting transfers between devices: 17.8 us -> none  [the longest x1 5.2 us: shards(): lax.all_to_all(cell_list, 'strike', split_axis=0, concat_axis=0, tiled=True)]
  transfers between devices with their start and end apart: 21 -> 0, of which waited for: 10 -> 0; matrix products, arithmetic and copies ran while one was open for 15% -> 0% of each run, Pallas kernels for 0% -> 0%
where the time goes in v1:
time: 33.3 us; the launch traced here: 33.1 us
  Pallas kernels  30 us (90%)
  local copies, waits for them, and re-layouts  2.48 us (7%)
  between operations  0.65 us (2%)
    pallas_call x1, Pallas kernels, shards(): pl.pallas_call(functools.partial(kernel, strike_count, dip_count, slot_co...  30 us
    unnamed x4, local copies, waits for them, and re-layouts  2.48 us

profile of v1, /device:TPU:0, one launch (start us, length us, event | category | flops | bytes accessed | tf_op | source)
XLA Modules:
  0.0 33.1 jit_solution(7733756502668728495)
XLA Ops:
  0.6 30.0 %adjoint.1 = (f32[9,8,16,128]{3,2,1,0:T(8,128)}, f32[2,64]{1,0:T(2,128)}) custom-call(f32[9,8,16,128]{3,2,1,0:T(8,128)} %state.1, f32[8,16,128]{2,1,0:T(8,128)} %lam.1, f32[8,16,128]{2,1,0:T(8,128)} %mu.1, f32[8,16,128]{2,1,0:T(8,128)} %buoy.1, bf16[3,512,128]{2,1,0:T(8,128)(2,1)} %bitcast.4, s32[1,512]{1,0:T(1,128)} %bitcast.6, s32[1,512]{1,0:T(1,128)} %bitcast.7, ...), custom_call_target="tpu_custom_call" | custom-call | tf_op jit(solution)/shard_map/adjoint/pallas_call | solution.py:391
  30.6 0.0 copy-start
  30.7 1.9 %copy.17 = f32[9,8,16,128]{3,2,1,0:T(8,128)} copy(f32[9,8,16,128]{3,2,1,0:T(8,128)} %get-tuple-element.4) | data formatting | bytes 1179648
  32.6 0.0 copy-done
  32.6 0.6 %copy.18 = f32[2,64]{1,0:T(2,128)} copy(f32[2,64]{1,0:T(2,128)S(1)} %copy-done) | data formatting | bytes 1024
Async XLA Ops:
  30.6 1.9 %copy-start = (f32[2,64]{1,0:T(2,128)S(1)}, f32[2,64]{1,0:T(2,128)}, u32[]{:S(2)}) copy-start(f32[2,64]{1,0:T(2,128)} %get-tuple-element.5) | copy-start | bytes 1540

commit v2 on v1

--- a/solution.py
+++ b/solution.py
@@ -55,45 +55,37 @@
     return (after - before) * 0.5
 
 
-def kernel(
-    strike_count,
-    dip_count,
-    slot_count,
-    state,
-    lam,
-    mu,
-    buoy,
-    residual,
-    tiles,
-    cells,
-    resample,
-    patch,
-    fault_cell,
-    area,
-    moment,
-    order,
-    out,
-    slip,
-    packed,
-    landed,
-    source,
-    onehot_hi,
-    picks,
-    sums_out,
-    sums_in,
-    x_out,
-    x_low,
-    x_high,
-    y_out,
-    y_low,
-    y_high,
-    route_send,
-    route_recv,
-    sum_send,
-    sum_recv,
-    halo_send,
-    halo_recv,
-):
+def kernel(strike_count, dip_count, slot_count, *refs):
+    (far, refs) = (refs[:13], refs[13:])
+    (out, slip), refs = refs[:2], refs[2:]
+    near, refs = refs[:13], refs[13:]
+    state, lam, mu, buoy, residual, tiles, cells, resample, patch, fault_cell, area, moment, order = near
+    (
+        packed,
+        landed,
+        middle,
+        arrived,
+        source,
+        onehot_hi,
+        picks,
+        sums_out,
+        sums_in,
+        x_out,
+        x_low,
+        x_high,
+        y_out,
+        y_low,
+        y_high,
+        fetch_sem,
+        dip_send,
+        dip_recv,
+        strike_send,
+        strike_recv,
+        sum_send,
+        sum_recv,
+        halo_send,
+        halo_recv,
+    ) = refs
     count = strike_count * dip_count
     strike = lax.axis_index("strike")
     dip = lax.axis_index("dip")
@@ -103,9 +95,8 @@
     stations = residual.shape[1]
     steps = resample.shape[0]
     shift = size_z.bit_length() - 1
-    slots = count * slot_count
-    groups = slots // LANES
-    per_group = LANES // slot_count
+    width = packed.shape[2]
+    slots = strike_count * LANES
     owned = order.shape[1] // count
     per_block = LANES // owned
     blocks = order.shape[1] // LANES
@@ -116,12 +107,31 @@
 
     barrier = pltpu.get_barrier_semaphore()
 
-    def greet(k, carry):
-        _, device = peer(k)
-        pl.semaphore_signal(barrier, inc=1, device_id=device, device_id_type=MESH)
-        return carry
-
-    lax.fori_loop(1, count, greet, 0)
+    def dip_peer(k):
+        to = lax.rem(dip + k, dip_count)
+        return to, (strike, to)
+
+    def strike_peer(k):
+        to = lax.rem(strike + k, strike_count)
+        return to, (to, dip)
+
+    def greet(which):
+        def one(k, carry):
+            pl.semaphore_signal(barrier, inc=1, device_id=which(k)[1], device_id_type=MESH)
+            return carry
+
+        return one
+
+    lax.fori_loop(1, dip_count, greet(dip_peer), 0)
+    lax.fori_loop(1, strike_count, greet(strike_peer), 0)
+
+    fetches = [pltpu.make_async_copy(far[i], near[i], fetch_sem.at[i]) for i in range(13)]
+    early = (5, 6, 7, 4)
+    for i in early:
+        fetches[i].start()
+    for i in range(13):
+        if i not in early:
+            fetches[i].start()
 
     sides = (
         (strike > 0, (strike - 1, dip)),
@@ -183,7 +193,8 @@
         pl.when(jnp.logical_not(sides[side][0]))(clear)
 
     stress_x, stress_y = (3, 6, 7), (6, 4, 8)
-    stage(0, stress_x, stress_y)
+    for i in early:
+        fetches[i].wait()
 
     res_hi, res_lo = split(resample[...])
     weights = jnp.concatenate([res_hi, res_lo], axis=0)
@@ -201,31 +212,36 @@
         0.0,
     ).astype(jnp.bfloat16)
     ordinal = jnp.sum(named.astype(jnp.float32) * matmul(named, earlier), axis=0, keepdims=True)
-    slot_row = tile_row * slot_count + ordinal.astype(jnp.int32)
-    placing = one_hot((slots, stations), 0, slot_row)
+    slot_row = lax.rem(tile_row, dip_count) * width + (tile_row // dip_count) * slot_count + ordinal.astype(jnp.int32)
+    placing = one_hot((dip_count * width, stations), 0, slot_row)
     val_hi, val_lo = split(values)
     placed = matmul_nt(jnp.concatenate([val_hi, val_lo], axis=0), placing)
     placed = placed[:8] + placed[8:]
-    for g in range(groups):
-        packed[g] = placed[:, g * LANES : (g + 1) * LANES]
-
-    pl.semaphore_wait(barrier, count - 1)
-    send(0)
-
-    def route(k, carry):
-        to, device = peer(k)
+    for p in range(dip_count):
+        packed[p] = placed[:, p * width : (p + 1) * width]
+    fetches[0].wait()
+    stage(0, stress_x, stress_y)
+
+    pl.semaphore_wait(barrier, dip_count + strike_count - 2)
+
+    def route_dip(k, carry):
+        to, device = dip_peer(k)
         pltpu.make_async_remote_copy(
-            src_ref=packed.at[to // per_group],
-            dst_ref=landed.at[me],
-            send_sem=route_send,
-            recv_sem=route_recv,
+            src_ref=packed.at[to],
+            dst_ref=landed.at[dip],
+            send_sem=dip_send,
+            recv_sem=dip_recv,
             device_id=device,
             device_id_type=MESH,
         ).start()
         return carry
 
-    lax.fori_loop(1, count, route, 0)
-    landed[me] = packed[me // per_group]
+    lax.fori_loop(1, dip_count, route_dip, 0)
+    send(0)
+    landed[dip] = packed[dip]
+    for i in range(1, 13):
+        if i not in early:
+            fetches[i].wait()
 
     patch_row = patch[...]
     entries = patch_row.shape[1]
@@ -257,7 +273,7 @@
             old = (out if turn else state)[c]
             moved = old + force(turn, c, rhs[c])
             if step:
-                moved = moved + time_step * source[step * 3 + c].reshape(size_x, size_y, size_z)
+                moved = moved + source[(step - 1) * 3 + c].reshape(size_x, size_y, size_z)
             out[c] = moved
 
     def stress(turn, first):
@@ -286,34 +302,54 @@
             total = taken if total is None else total + taken
         return jnp.sum(total * onehot_hi[...], axis=0, keepdims=True)
 
+    from_dip = landed.at[pl.ds(0, dip_count - 1)]
+    pltpu.make_async_copy(from_dip, from_dip, dip_recv).wait()
+    lane = lax.broadcasted_iota(jnp.int32, (8, LANES), 1) // slot_count
+    for t in range(strike_count):
+        block, offset = divmod(t * slot_count, LANES)
+        total = jnp.zeros((8, LANES), jnp.float32)
+        for j in range(dip_count):
+            piece = landed[j, :, block * LANES : (block + 1) * LANES]
+            turn = (j * slot_count - offset) % LANES
+            total = jnp.where(lane == j, pltpu.roll(piece, turn, 1) if turn else piece, total)
+        middle[t] = total
+
+    def route_strike(k, carry):
+        to, device = strike_peer(k)
+        pltpu.make_async_remote_copy(
+            src_ref=middle.at[to],
+            dst_ref=arrived.at[strike],
+            send_sem=strike_send,
+            recv_sem=strike_recv,
+            device_id=device,
+            device_id_type=MESH,
+        ).start()
+        return carry
+
+    lax.fori_loop(1, strike_count, route_strike, 0)
+    arrived[strike] = middle[strike]
+    pltpu.make_async_copy(from_dip, from_dip, dip_send).wait()
+
     receive(0)
     velocity(0, 0)
 
-    all_landed = landed.at[pl.ds(0, count - 1)]
-    pltpu.make_async_copy(all_landed, all_landed, route_recv).wait()
-    pltpu.make_async_copy(all_landed, all_landed, route_send).wait()
-    mine = lax.rem(me, per_group)
-    lane = lax.broadcasted_iota(jnp.int32, (8, LANES), 1)
-    gathered = []
-    for g in range(groups):
-        total = jnp.zeros((8, LANES), jnp.float32)
-        for j in range(per_group):
-            turned = pltpu.roll(landed[g * per_group + j], lax.rem(j - mine + per_group, per_group) * slot_count, 1)
-            total = jnp.where(lane // slot_count == j, turned, total)
-        gathered.append(total)
-    arrived = jnp.concatenate(gathered, axis=1)
-    hi_ids = arrived[6:7].astype(jnp.int32)
-    lo_ids = arrived[7:8].astype(jnp.int32)
+    from_strike = arrived.at[pl.ds(0, strike_count - 1)]
+    pltpu.make_async_copy(from_strike, from_strike, strike_recv).wait()
+    inbox = jnp.concatenate([arrived[g] for g in range(strike_count)], axis=1)
+    hi_ids = inbox[6:7].astype(jnp.int32)
+    lo_ids = inbox[7:8].astype(jnp.int32)
     spread_lo = one_hot((size_z, slots), 0, lo_ids)
     row_mask = lax.broadcasted_iota(jnp.int32, (rows, slots), 0) == hi_ids
-    amp_hi, amp_lo = split(arrived)
+    amp_hi, amp_lo = split(inbox)
     amp_hi, amp_lo = amp_hi.astype(jnp.float32), amp_lo.astype(jnp.float32)
-    for m in range(steps * 3):
+
+    def injected(m):
         high = jnp.where(row_mask, amp_hi[m : m + 1], 0.0).astype(jnp.bfloat16)
         low = jnp.where(row_mask, amp_lo[m : m + 1], 0.0).astype(jnp.bfloat16)
-        source[m] = matmul_nt(high, spread_lo) + matmul_nt(low, spread_lo)
+        return time_step * (matmul_nt(high, spread_lo) + matmul_nt(low, spread_lo))
+
     for c in range(3):
-        out[c] = out[c] + time_step * source[c].reshape(size_x, size_y, size_z)
+        out[c] = out[c] + injected(c).reshape(size_x, size_y, size_z)
 
     flow = (0, 1, 2)
     contribs = []
@@ -323,6 +359,10 @@
             velocity(2 * step, step)
         stage(2 * step + 1, flow, flow)
         send(2 * step + 1)
+        if step == 0:
+            for m in range(3, steps * 3):
+                source[m - 3] = injected(m)
+            pltpu.make_async_copy(from_strike, from_strike, strike_send).wait()
         receive(2 * step + 1)
         stress(2 * step + 1, step == 0)
         if step < steps - 1:
@@ -382,44 +422,15 @@
     steps = resample.shape[0]
     size_x, size_y, size_z = buoyancy.shape
     rows = size_x * size_y
-    slots = count * slot_count
+    width = -(-strike_count * slot_count // LANES) * LANES
+    assert dip_count * slot_count <= LANES
     entries = fault_patch.shape[1]
     patches = moment.shape[1]
     turns = 2 * steps
+    anywhere = pl.BlockSpec(memory_space=pl.ANY)
     vmem = pl.BlockSpec(memory_space=pltpu.VMEM)
     f32, bf16 = jnp.float32, jnp.bfloat16
-    return pl.pallas_call(
-        functools.partial(kernel, strike_count, dip_count, slot_count),
-        out_shape=(
-            jax.ShapeDtypeStruct(adjoint_state.shape, f32),
-            jax.ShapeDtypeStruct((steps, patches // count), f32),
-        ),
-        in_specs=[vmem] * 13,
-        out_specs=(vmem, vmem),
-        scratch_shapes=[
-            pltpu.VMEM((slots // LANES, 8, LANES), f32),
-            pltpu.VMEM((count, 8, LANES), f32),
-            pltpu.VMEM((steps * 3, rows, size_z), f32),
-            pltpu.VMEM((rows, entries), f32),
-            pltpu.VMEM((entries, patches), bf16),
-            pltpu.VMEM((patches // LANES, steps, LANES), f32),
-            pltpu.VMEM((count, steps, LANES), f32),
-            pltpu.VMEM((turns, 2, 3, size_y, size_z), f32),
-            pltpu.VMEM((turns, 3, size_y, size_z), f32),
-            pltpu.VMEM((turns, 3, size_y, size_z), f32),
-            pltpu.VMEM((turns, 2, 3, size_x, 1, size_z), f32),
-            pltpu.VMEM((turns, 3, size_x, 1, size_z), f32),
-            pltpu.VMEM((turns, 3, size_x, 1, size_z), f32),
-            pltpu.SemaphoreType.DMA,
-            pltpu.SemaphoreType.DMA,
-            pltpu.SemaphoreType.DMA,
-            pltpu.SemaphoreType.DMA,
-            pltpu.SemaphoreType.DMA((turns, 4)),
-            pltpu.SemaphoreType.DMA((turns, 4)),
-        ],
-        compiler_params=pltpu.CompilerParams(collective_id=0, has_side_effects=True),
-        name="adjoint",
-    )(
+    operands = (
         adjoint_state,
         lame_lambda,
         lame_mu,
@@ -434,6 +445,44 @@
         moment,
         subpatch_order.reshape(1, -1),
     )
+    return pl.pallas_call(
+        functools.partial(kernel, strike_count, dip_count, slot_count),
+        out_shape=(
+            pltpu.VMEM(adjoint_state.shape, f32),
+            pltpu.VMEM((steps, patches // count), f32),
+        ),
+        in_specs=[anywhere] * 13,
+        out_specs=(vmem, vmem),
+        scratch_shapes=[
+            *(pltpu.VMEM(a.shape, a.dtype) for a in operands),
+            pltpu.VMEM((dip_count, 8, width), f32),
+            pltpu.VMEM((dip_count, 8, width), f32),
+            pltpu.VMEM((strike_count, 8, LANES), f32),
+            pltpu.VMEM((strike_count, 8, LANES), f32),
+            pltpu.VMEM((steps * 3 - 3, rows, size_z), f32),
+            pltpu.VMEM((rows, entries), f32),
+            pltpu.VMEM((entries, patches), bf16),
+            pltpu.VMEM((patches // LANES, steps, LANES), f32),
+            pltpu.VMEM((count, steps, LANES), f32),
+            pltpu.VMEM((turns, 2, 3, size_y, size_z), f32),
+            pltpu.VMEM((turns, 3, size_y, size_z), f32),
+            pltpu.VMEM((turns, 3, size_y, size_z), f32),
+            pltpu.VMEM((turns, 2, 3, size_x, 1, size_z), f32),
+            pltpu.VMEM((turns, 3, size_x, 1, size_z), f32),
+            pltpu.VMEM((turns, 3, size_x, 1, size_z), f32),
+            pltpu.SemaphoreType.DMA((13,)),
+            pltpu.SemaphoreType.DMA,
+            pltpu.SemaphoreType.DMA,
+            pltpu.SemaphoreType.DMA,
+            pltpu.SemaphoreType.DMA,
+            pltpu.SemaphoreType.DMA,
+            pltpu.SemaphoreType.DMA,
+            pltpu.SemaphoreType.DMA((turns, 4)),
+            pltpu.SemaphoreType.DMA((turns, 4)),
+        ],
+        compiler_params=pltpu.CompilerParams(collective_id=0, has_side_effects=True),
+        name="adjoint",
+    )(*operands)
 
 
 def solution(mesh):

time: 33.3 us -> 29.6 us (0.89)
  Pallas kernels: 30 us -> 27.4 us
  local copies, waits for them, and re-layouts: 2.48 us -> 1.38 us
    pallas_call x1, Pallas kernels: 30 us -> 27.4 us  [shards(): pl.pallas_call(functools.partial(kernel, strike_count, dip_count, slot_co...]
    unnamed x4 -> x2, local copies, waits for them, and re-layouts: 2.48 us -> 1.38 us
where the time goes in v2:
time: 29.6 us; the launch traced here: 29.5 us
  Pallas kernels  27.4 us (93%)
  local copies, waits for them, and re-layouts  1.38 us (5%)
  between operations  0.64 us (2%)
    pallas_call x1, Pallas kernels, shards(): pl.pallas_call(functools.partial(kernel, strike_count, dip_count, slot_co...  27.4 us
    unnamed x2, local copies, waits for them, and re-layouts  1.38 us

profile of v2, /device:TPU:0, one launch (start us, length us, event | category | flops | bytes accessed | tf_op | source)
XLA Modules:
  0.0 29.5 jit_solution(2113245920561016583)
XLA Ops:
  0.6 27.4 %adjoint.1 = (f32[9,8,16,128]{3,2,1,0:T(8,128)S(1)}, f32[2,64]{1,0:T(2,128)S(1)}) custom-call(f32[9,8,16,128]{3,2,1,0:T(8,128)} %refs_0_.1, f32[8,16,128]{2,1,0:T(8,128)} %refs_1_.1, f32[8,16,128]{2,1,0:T(8,128)} %refs_2_.1, f32[8,16,128]{2,1,0:T(8,128)} %refs_3_.1, bf16[3,512,128]{2,1,0:T(8,128)(2,1)} %bitcast.4, s32[1,512]{1,0:T(1,128)} %bitcast.6, ...), custom_call_target="tpu_custom_call" | custom-call | tf_op jit(solution)/shard_map/adjoint/pallas_call | solution.py:448
  28.1 0.8 %copy.17 = f32[9,8,16,128]{3,2,1,0:T(8,128)} copy(f32[9,8,16,128]{3,2,1,0:T(8,128)S(1)} %get-tuple-element.2) | data formatting | bytes 1179648
  28.9 0.6 %copy.18 = f32[2,64]{1,0:T(2,128)} copy(f32[2,64]{1,0:T(2,128)S(1)} %get-tuple-element.3) | data formatting | bytes 1024

commit v3 on v2

--- a/solution.py
+++ b/solution.py
@@ -176,7 +176,6 @@
         for side, copy in enumerate(halo_copies(turn)):
 
             def finish(turn=turn, side=side, copy=copy):
-                copy.wait_send()
                 sender, low, high = halves[side // 2]
                 target = low if side % 2 == 0 else high
                 pltpu.make_async_copy(target.at[turn], target.at[turn], halo_recv.at[turn, side]).wait()
@@ -328,8 +327,6 @@
 
     lax.fori_loop(1, strike_count, route_strike, 0)
     arrived[strike] = middle[strike]
-    pltpu.make_async_copy(from_dip, from_dip, dip_send).wait()
-
     receive(0)
     velocity(0, 0)
 
@@ -362,7 +359,6 @@
         if step == 0:
             for m in range(3, steps * 3):
                 source[m - 3] = injected(m)
-            pltpu.make_async_copy(from_strike, from_strike, strike_send).wait()
         receive(2 * step + 1)
         stress(2 * step + 1, step == 0)
         if step < steps - 1:
@@ -392,11 +388,25 @@
     sums_in[me] = sums_out[me // per_block]
     all_sums = sums_in.at[pl.ds(0, count - 1)]
     pltpu.make_async_copy(all_sums, all_sums, sum_recv).wait()
-    pltpu.make_async_copy(all_sums, all_sums, sum_send).wait()
     final = jnp.sum(sums_in[...], axis=0)
     final = jnp.concatenate([final, jnp.zeros((8 - steps, LANES), jnp.float32)], axis=0)
     first = lax.rem(me, per_block) * owned
     slip[...] = pltpu.roll(final, lax.rem(LANES - first, LANES), 1)[:steps, :owned]
+
+    pltpu.make_async_copy(from_dip, from_dip, dip_send).wait()
+    pltpu.make_async_copy(from_strike, from_strike, strike_send).wait()
+    pltpu.make_async_copy(all_sums, all_sums, sum_send).wait()
+    for turn in range(2 * steps):
+        for side, copy in enumerate(halo_copies(turn)):
+            pl.when(sides[side][0])(copy.wait_send)
+
+
+def put(state, slip, out, grad, sems):
+    copies = [pltpu.make_async_copy(state, out, sems.at[0]), pltpu.make_async_copy(slip, grad, sems.at[1])]
+    for copy in copies:
+        copy.start()
+    for copy in copies:
+        copy.wait()
 
 
 def shards(
@@ -445,7 +455,7 @@
         moment,
         subpatch_order.reshape(1, -1),
     )
-    return pl.pallas_call(
+    state, slip = pl.pallas_call(
         functools.partial(kernel, strike_count, dip_count, slot_count),
         out_shape=(
             pltpu.VMEM(adjoint_state.shape, f32),
@@ -483,6 +493,19 @@
         compiler_params=pltpu.CompilerParams(collective_id=0, has_side_effects=True),
         name="adjoint",
     )(*operands)
+    state = pltpu.with_memory_space_constraint(state, pltpu.VMEM)
+    slip = pltpu.with_memory_space_constraint(slip, pltpu.VMEM)
+    return pl.pallas_call(
+        put,
+        out_shape=(
+            jax.ShapeDtypeStruct(state.shape, f32),
+            jax.ShapeDtypeStruct(slip.shape, f32),
+        ),
+        in_specs=[vmem, vmem],
+        out_specs=(anywhere, anywhere),
+        scratch_shapes=[pltpu.SemaphoreType.DMA((2,))],
+        name="put",
+    )(state, slip)
 
 
 def solution(mesh):

time: 29.6 us -> 29.1 us (0.983)
  local copies, waits for them, and re-layouts: 1.38 us -> 0 us
  Pallas kernels: 27.4 us -> 28.3 us
    unnamed x2 -> x0, local copies, waits for them, and re-layouts: 1.38 us -> none
    pallas_call x0 -> x1, Pallas kernels: none -> 0.84 us  [shards(): pl.pallas_call(put, out_shape=(jax.ShapeDtypeStruct(state.shape, f32), ja...]
where the time goes in v3:
time: 29.1 us; the launch traced here: 28.9 us
  Pallas kernels  28.3 us (97%)
  between operations  0.64 us (2%)
    pallas_call x1, Pallas kernels, shards(): pl.pallas_call(functools.partial(kernel, strike_count, dip_count, slot_co...  27.5 us
    pallas_call x1, Pallas kernels, shards(): pl.pallas_call(put, out_shape=(jax.ShapeDtypeStruct(state.shape, f32), ja...  0.84 us

profile of v3, /device:TPU:0, one launch (start us, length us, event | category | flops | bytes accessed | tf_op | source)
XLA Modules:
  0.0 28.9 jit_solution(6304236047504365161)
XLA Ops:
  0.6 27.5 %adjoint.1 = (f32[9,8,16,128]{3,2,1,0:T(8,128)S(1)}, f32[2,64]{1,0:T(2,128)S(1)}) custom-call(f32[9,8,16,128]{3,2,1,0:T(8,128)} %refs_0_.1, f32[8,16,128]{2,1,0:T(8,128)} %refs_1_.1, f32[8,16,128]{2,1,0:T(8,128)} %refs_2_.1, f32[8,16,128]{2,1,0:T(8,128)} %refs_3_.1, bf16[3,512,128]{2,1,0:T(8,128)(2,1)} %bitcast.4, s32[1,512]{1,0:T(1,128)} %bitcast.6, ...), custom_call_target="tpu_custom_call" | custom-call | tf_op jit(solution)/shard_map/adjoint/pallas_call | solution.py:458
  28.1 0.8 %put.1 = (f32[9,8,16,128]{3,2,1,0:T(8,128)}, f32[2,64]{1,0:T(2,128)}) custom-call(f32[9,8,16,128]{3,2,1,0:T(8,128)S(1)} %get-tuple-element.4.state, f32[2,64]{1,0:T(2,128)S(1)} %get-tuple-element.5.slip), custom_call_target="tpu_custom_call" | custom-call | tf_op jit(solution)/shard_map/put/pallas_call | solution.py:498
